TPU v7x, 128 devices: a whole 4x4x4 slice. The times are simulated.
128 devices in a mesh: segment: 4 (over y), lane: 32 (over x, z, core).
Axes of the slice: x: 4, y: 4, z: 4, core: 2. Of those that a mesh axis runs over, the one named last changes fastest.
Arguments:
- frames: bfloat16 [96, 197, 1024], P('lane'), may hold values from -6 to 6
- triple_weight: bfloat16 [4, 1024, 3072], P('segment'), as said below
- output_weight: bfloat16 [4, 1024, 1024], P('segment'), may hold values from -0.1875 to 0.1875
- expand_weight: bfloat16 [4, 1024, 4096], P('segment', None, 'lane'), may hold values from -0.1875 to 0.1875
- reduce_weight: bfloat16 [4, 4096, 1024], P('segment', 'lane'), may hold values from -0.09375 to 0.09375
- attend_gain: float32 [4, 1024], P('segment'), may hold values from 0.1 to 1.9
- dense_gain: float32 [4, 1024], P('segment'), may hold values from 0.1 to 1.9
- final_gain: float32 [1024], replicated, may hold values from 0.1 to 1.9
- shot_lengths: int32 [24], replicated, may hold values from 1 to 12, as said below
Outputs:
- shot_frames: float32 [96, 1024], P('lane', 'segment')
Inputs may be any that keep to these rules, and one draw needn't show every extreme that they name: `shot_lengths`: each shot is a run of consecutive frames; the lengths sum to 96; the first shot has 2 frames and the second exactly 12. `triple_weight`: query and value columns are drawn like a weight with fan-in 1024; key columns may be up to 60 times that scale and correlated with the query columns.
All inputs are finite; a program needn't handle non-finite values.
Results may differ from a plain program's by a relative error of at most 0.023.
Values may be sent and summed in bfloat16 or wider, within the bound.
A program may use at most 128 MiB of HBM per device.

v0:
```python
import math
import jax
import jax.numpy as jnp
from jax import lax
from jax.sharding import PartitionSpec as P

HEADS = 16
MOST = 12


def from_behind(value, axis, steps):
    count = lax.axis_size(axis)
    leading, last = (max(0, -steps), min(count, count - steps))
    return lax.ppermute(value, axis, [(source, source + steps) for source in range(leading, last)])


def normalize(states, gain_row):
    average = jnp.mean(states, axis=-1, keepdims=True)
    centred = states - average
    spread = jnp.mean(centred * centred, axis=-1, keepdims=True)
    return centred * lax.rsqrt(spread + 1e-06) * gain_row


def spatial_layer(
    states, triple_weight, output_weight, expand_weight, reduce_weight, attend_gain, dense_gain
):
    group_size, row_count, model_width = states.shape
    head_size = model_width // HEADS
    normed = normalize(states, attend_gain).astype(jnp.bfloat16)
    packed = jnp.einsum(
        "gpd,de->gpe", normed, triple_weight, preferred_element_type=jnp.float32
    ).astype(jnp.bfloat16)
    packed = packed.reshape(group_size, row_count, 3, HEADS, head_size)
    scores = jnp.einsum(
        "gqhe,gkhe->ghqk", packed[:, :, 0], packed[:, :, 1], preferred_element_type=jnp.float32
    ) / math.sqrt(head_size)
    weights = jax.nn.softmax(scores, axis=-1).astype(jnp.bfloat16)
    context = jnp.einsum(
        "ghqk,gkhe->gqhe", weights, packed[:, :, 2], preferred_element_type=jnp.float32
    )
    context = context.astype(jnp.bfloat16).reshape(group_size, row_count, model_width)
    states = states + jnp.einsum(
        "gpd,de->gpe", context, output_weight, preferred_element_type=jnp.float32
    )
    normed = normalize(states, dense_gain).astype(jnp.bfloat16)
    hidden = jax.nn.gelu(
        jnp.einsum("gpd,df->gpf", normed, expand_weight, preferred_element_type=jnp.float32),
        approximate=False,
    ).astype(jnp.bfloat16)
    return states + jnp.einsum(
        "gpf,fd->gpd", hidden, reduce_weight, preferred_element_type=jnp.float32
    )


def shot_number(positions, shot_ends):
    return jnp.sum((shot_ends[None, :] <= positions[:, None]).astype(jnp.int32), axis=1)


def fold_keys(running, portion, first_row, queries, query_shot, shot_ends, frame_total):
    highest, totals, weighted = running
    row_count = portion.shape[0]
    model_width = portion.shape[1] // 2
    head_size = model_width // HEADS
    key_rows = portion[:, :model_width].reshape(row_count, HEADS, head_size)
    value_rows = portion[:, model_width:].astype(jnp.float32).reshape(row_count, HEADS, head_size)
    positions = first_row + jnp.arange(row_count, dtype=jnp.int32)
    inside = (positions >= 0) & (positions < frame_total)
    allowed = (query_shot[:, None] == shot_number(positions, shot_ends)[None, :]) & inside[None, :]
    scores = jnp.einsum(
        "qhe,khe->hqk", queries, key_rows, preferred_element_type=jnp.float32
    ) / math.sqrt(head_size)
    masked = jnp.where(allowed[None], scores, -1e30)
    raised = jnp.maximum(highest, jnp.max(masked, axis=-1))
    factor = jnp.exp(highest - raised)
    shares = jnp.where(allowed[None], jnp.exp(scores - raised[:, :, None]), 0.0)
    totals = totals * factor + jnp.sum(shares, axis=-1)
    weighted = weighted * jnp.transpose(factor)[:, :, None] + jnp.einsum(
        "hqk,khe->qhe", shares, value_rows, precision=lax.Precision.HIGHEST
    )
    return (raised, totals, weighted)


def body(
    frames,
    triple_weight,
    output_weight,
    expand_weight,
    reduce_weight,
    attend_gain,
    dense_gain,
    final_gain,
    shot_lengths,
):
    segment_index = lax.axis_index("segment")
    segment_count = lax.axis_size("segment")
    lane_index = lax.axis_index("lane")
    lane_count = lax.axis_size("lane")
    frame_count, row_count, model_width = frames.shape
    expand_full, reduce_full = (
        lax.all_gather(expand_weight[0], "lane", axis=1, tiled=True),
        lax.all_gather(reduce_weight[0], "lane", axis=0, tiled=True),
    )
    triple_local = triple_weight[0]
    output_local = output_weight[0]
    attend_local = attend_gain[0]
    dense_local = dense_gain[0]
    group_size = 1
    micro_count = frame_count // group_size

    def advance(moment, running):
        current, pooled = running
        first_frame = jnp.minimum(moment, micro_count - 1) * group_size
        loaded = lax.dynamic_slice_in_dim(frames, first_frame, group_size, 0).astype(jnp.float32)
        current = jnp.where(segment_index == 0, loaded, current)
        result = spatial_layer(
            current, triple_local, output_local, expand_full, reduce_full, attend_local, dense_local
        )
        arrived = from_behind(result, "segment", 1)
        finished = moment - (segment_count - 2)
        summary = jnp.mean(normalize(arrived, final_gain), axis=1)
        slot_row = jnp.clip(finished, 0, micro_count - 1) * group_size
        previous = lax.dynamic_slice_in_dim(pooled, slot_row, group_size, 0)
        updated = jnp.where(finished >= 0, summary, previous)
        return (arrived, lax.dynamic_update_slice_in_dim(pooled, updated, slot_row, 0))

    start_state = (
        jnp.zeros((group_size, row_count, model_width), jnp.float32),
        jnp.zeros((frame_count, model_width), jnp.float32),
    )
    settled, pooled = lax.fori_loop(0, micro_count + segment_count - 2, advance, start_state)
    head_size = model_width // HEADS
    normed = normalize(pooled, attend_local).astype(jnp.bfloat16)
    packed = jnp.dot(normed, triple_local, preferred_element_type=jnp.float32).astype(jnp.bfloat16)
    queries = packed[:, :model_width].reshape(frame_count, HEADS, head_size)
    key_value = packed[:, model_width:]
    shot_ends = jnp.cumsum(shot_lengths)
    frame_total = frame_count * lane_count
    own_rows = lane_index * frame_count + jnp.arange(frame_count, dtype=jnp.int32)
    query_shot = shot_number(own_rows, shot_ends)

    def absorb(running, portion, first_row):
        return fold_keys(running, portion, first_row, queries, query_shot, shot_ends, frame_total)

    empty = (
        jnp.full((HEADS, frame_count), -1e30, jnp.float32),
        jnp.zeros((HEADS, frame_count), jnp.float32),
        jnp.zeros((frame_count, HEADS, head_size), jnp.float32),
    )
    running = absorb(empty, key_value, lane_index * frame_count)
    reach = (MOST + frame_count - 2) // frame_count
    offsets = [direction * distance for distance in range(1, reach + 1) for direction in (1, -1)]
    for offset in offsets:
        portion = from_behind(key_value, "lane", offset)
        running = absorb(running, portion, (lane_index - offset) * frame_count)
    highest, totals, weighted = running
    context = (
        (weighted / jnp.transpose(totals)[:, :, None])
        .reshape(frame_count, model_width)
        .astype(jnp.bfloat16)
    )
    temporal = pooled + jnp.dot(context, output_local, preferred_element_type=jnp.float32)
    normed = normalize(temporal, dense_local).astype(jnp.bfloat16)
    hidden = jax.nn.gelu(
        jnp.dot(normed, expand_full, preferred_element_type=jnp.float32), approximate=False
    ).astype(jnp.bfloat16)
    temporal = temporal + jnp.dot(hidden, reduce_full, preferred_element_type=jnp.float32)
    columns = temporal.reshape(frame_count, segment_count, model_width // segment_count)
    shared = lax.all_to_all(columns, "segment", split_axis=1, concat_axis=1, tiled=True)
    return shared[:, segment_count - 1]


def solution(mesh):
    return jax.shard_map(
        body,
        mesh=mesh,
        in_specs=(
            P("lane", None, None),
            P("segment", None, None),
            P("segment", None, None),
            P("segment", None, "lane"),
            P("segment", "lane", None),
            P("segment", None),
            P("segment", None),
            P(),
            P(),
        ),
        out_specs=P("lane", "segment"),
        check_vma=False,
    )
```

profile of v0, /device:TPU:2, one launch (start us, length us, event | category | flops | bytes accessed | tf_op | source)
XLA Modules:
  0.0 478.3 jit_solution(12670992070367799868)
XLA Ops:
  10.1 61.2 %all-gather.5.cloned.1.call-done = bf16[1,1024,4096]{2,1,0:T(8,128)(2,1)} async-done(((bf16[1,1024,128]{2,1,0:T(8,128)(2,1)}), bf16[1,1024,4096]{2,1,0:T(8,128)(2,1)}) %all-gather.5.cloned.1.call-update) | async-done | bytes 8388624 | tf_op jit(solution)/shard_map/all_gather | solution.py:100
  71.3 55.2 %all-gather.7.cloned.1.call-done = bf16[1,4096,1024]{2,1,0:T(8,128)(2,1)} async-done(((bf16[1,128,1024]{2,1,0:T(8,128)(2,1)}), bf16[1,4096,1024]{2,1,0:T(8,128)(2,1)}) %all-gather.7.cloned.1.call-update) | async-done | bytes 8388624 | tf_op jit(solution)/shard_map/all_gather | solution.py:101
  127.0 283.0 %while.17 = (s32[]{:T(128)}, f32[1,197,1024]{2,0,1:T(1,128)S(1)}, f32[3,1024]{1,0:T(4,128)S(1)}, pred[]{:T(512)}, bf16[3,197,1024]{2,1,0:T(8,128)(2,1)}, /*index...) while((s32[]{:T(128)}, f32[1,197,1024]{2,0,1:T(1,128)S(1)}, ...), condition=%wide.region_10.11_spmd, body=%wide.region_0.10_spmd.sunk | while | flops 5180471808 | bytes 65759924 | solution.py:130
  129.5 5.6 %convolution_convert_fusion.3 = bf16[197,3072]{1,0:T(8,128)(2,1)} fusion(bf16[1024,3072]{1,0:T(8,128)(2,1)} %get-tuple-element.539, f32[1024]{0:T(1024)} %bitcast.303, f32[197]{0:T(256)S(1)} %add_rsqrt_fusion.8, f32[197]{0:T(256)S(1)} %broadcast_multiply_fusion.10, f32[1,197,1024]{2,0,1:T(1,128)S(1)} %get-tuple-element.516, ...), kind=kOutput, calls=%fused_computation.2.clone.1 | convolution fusion | flops 1241232384 | bytes 8724524 | tf_op jit(solution)/shard_map/while/body/eval_jaxpr/gpd,de->gpe/dot_general | solution.py:30
  137.4 2.7 fusion.341
  143.7 14.2 %fusion.344 = f32[1,197,1024]{2,1,0:T(8,128)S(1)} fusion(f32[1,197,1024]{2,1,0:T(8,128)S(1)} %get-tuple-element.495, bf16[4096,1024]{1,0:T(8,128)(2,1)} %get-tuple-element.543, bf16[1024,4096]{1,0:T(8,128)(2,1)} %get-tuple-element.542, f32[1024]{0:T(1024)S(1)} %bitcast.305, f32[197]{0:T(256)S(1)} %add_rsqrt_fusion.9, ...), kind=kOutput, calls=%fused_computation.61.clone.1 | convolution fusion | flops 3358569472 | bytes 18396712 | tf_op jit(solution)/shard_map/while/body/eval_jaxpr/gpf,fd->gpd/dot_general | solution.py:50
  158.8 3.4 collective-permute-start
  162.2 17.6 %collective-permute-done = f32[1,197,1024]{2,0,1:T(1,128)S(1)} collective-permute-done((f32[1,197,1024]{2,0,1:T(1,128)S(1)}, f32[1,197,1024]{2,0,1:T(1,128)S(1)}, u32[]{:S(2)}, u32[]{:S(2)}) %collective-permute-start) | collective-permute-done | bytes 806944 | tf_op jit(solution)/shard_map/while/body/eval_jaxpr/ppermute | solution.py:14
  187.0 5.6 %convolution_convert_fusion.3 = bf16[197,3072]{1,0:T(8,128)(2,1)} fusion(bf16[1024,3072]{1,0:T(8,128)(2,1)} %get-tuple-element.539, f32[1024]{0:T(1024)} %bitcast.303, f32[197]{0:T(256)S(1)} %add_rsqrt_fusion.8, f32[197]{0:T(256)S(1)} %broadcast_multiply_fusion.10, f32[1,197,1024]{2,0,1:T(1,128)S(1)} %get-tuple-element.516, ...), kind=kOutput, calls=%fused_computation.2.clone.1 | convolution fusion | flops 1241232384 | bytes 8724524 | tf_op jit(solution)/shard_map/while/body/eval_jaxpr/gpd,de->gpe/dot_general | solution.py:30
  201.2 14.2 %fusion.344 = f32[1,197,1024]{2,1,0:T(8,128)S(1)} fusion(f32[1,197,1024]{2,1,0:T(8,128)S(1)} %get-tuple-element.495, bf16[4096,1024]{1,0:T(8,128)(2,1)} %get-tuple-element.543, bf16[1024,4096]{1,0:T(8,128)(2,1)} %get-tuple-element.542, f32[1024]{0:T(1024)S(1)} %bitcast.305, f32[197]{0:T(256)S(1)} %add_rsqrt_fusion.9, ...), kind=kOutput, calls=%fused_computation.61.clone.1 | convolution fusion | flops 3358569472 | bytes 18396712 | tf_op jit(solution)/shard_map/while/body/eval_jaxpr/gpf,fd->gpd/dot_general | solution.py:50
  216.3 4.4 collective-permute-start
  220.7 16.8 %collective-permute-done = f32[1,197,1024]{2,0,1:T(1,128)S(1)} collective-permute-done((f32[1,197,1024]{2,0,1:T(1,128)S(1)}, f32[1,197,1024]{2,0,1:T(1,128)S(1)}, u32[]{:S(2)}, u32[]{:S(2)}) %collective-permute-start) | collective-permute-done | bytes 806944 | tf_op jit(solution)/shard_map/while/body/eval_jaxpr/ppermute | solution.py:14
  244.7 5.6 %convolution_convert_fusion.3 = bf16[197,3072]{1,0:T(8,128)(2,1)} fusion(bf16[1024,3072]{1,0:T(8,128)(2,1)} %get-tuple-element.539, f32[1024]{0:T(1024)} %bitcast.303, f32[197]{0:T(256)S(1)} %add_rsqrt_fusion.8, f32[197]{0:T(256)S(1)} %broadcast_multiply_fusion.10, f32[1,197,1024]{2,0,1:T(1,128)S(1)} %get-tuple-element.516, ...), kind=kOutput, calls=%fused_computation.2.clone.1 | convolution fusion | flops 1241232384 | bytes 8724524 | tf_op jit(solution)/shard_map/while/body/eval_jaxpr/gpd,de->gpe/dot_general | solution.py:30
  258.9 14.2 %fusion.344 = f32[1,197,1024]{2,1,0:T(8,128)S(1)} fusion(f32[1,197,1024]{2,1,0:T(8,128)S(1)} %get-tuple-element.495, bf16[4096,1024]{1,0:T(8,128)(2,1)} %get-tuple-element.543, bf16[1024,4096]{1,0:T(8,128)(2,1)} %get-tuple-element.542, f32[1024]{0:T(1024)S(1)} %bitcast.305, f32[197]{0:T(256)S(1)} %add_rsqrt_fusion.9, ...), kind=kOutput, calls=%fused_computation.61.clone.1 | convolution fusion | flops 3358569472 | bytes 18396712 | tf_op jit(solution)/shard_map/while/body/eval_jaxpr/gpf,fd->gpd/dot_general | solution.py:50
  274.0 4.4 collective-permute-start
  278.4 15.9 %collective-permute-done = f32[1,197,1024]{2,0,1:T(1,128)S(1)} collective-permute-done((f32[1,197,1024]{2,0,1:T(1,128)S(1)}, f32[1,197,1024]{2,0,1:T(1,128)S(1)}, u32[]{:S(2)}, u32[]{:S(2)}) %collective-permute-start) | collective-permute-done | bytes 806944 | tf_op jit(solution)/shard_map/while/body/eval_jaxpr/ppermute | solution.py:14
  301.5 5.6 %convolution_convert_fusion.3 = bf16[197,3072]{1,0:T(8,128)(2,1)} fusion(bf16[1024,3072]{1,0:T(8,128)(2,1)} %get-tuple-element.539, f32[1024]{0:T(1024)} %bitcast.303, f32[197]{0:T(256)S(1)} %add_rsqrt_fusion.8, f32[197]{0:T(256)S(1)} %broadcast_multiply_fusion.10, f32[1,197,1024]{2,0,1:T(1,128)S(1)} %get-tuple-element.516, ...), kind=kOutput, calls=%fused_computation.2.clone.1 | convolution fusion | flops 1241232384 | bytes 8724524 | tf_op jit(solution)/shard_map/while/body/eval_jaxpr/gpd,de->gpe/dot_general | solution.py:30
  315.7 14.2 %fusion.344 = f32[1,197,1024]{2,1,0:T(8,128)S(1)} fusion(f32[1,197,1024]{2,1,0:T(8,128)S(1)} %get-tuple-element.495, bf16[4096,1024]{1,0:T(8,128)(2,1)} %get-tuple-element.543, bf16[1024,4096]{1,0:T(8,128)(2,1)} %get-tuple-element.542, f32[1024]{0:T(1024)S(1)} %bitcast.305, f32[197]{0:T(256)S(1)} %add_rsqrt_fusion.9, ...), kind=kOutput, calls=%fused_computation.61.clone.1 | convolution fusion | flops 3358569472 | bytes 18396712 | tf_op jit(solution)/shard_map/while/body/eval_jaxpr/gpf,fd->gpd/dot_general | solution.py:50
  330.8 4.4 collective-permute-start
  335.2 14.9 %collective-permute-done = f32[1,197,1024]{2,0,1:T(1,128)S(1)} collective-permute-done((f32[1,197,1024]{2,0,1:T(1,128)S(1)}, f32[1,197,1024]{2,0,1:T(1,128)S(1)}, u32[]{:S(2)}, u32[]{:S(2)}) %collective-permute-start) | collective-permute-done | bytes 806944 | tf_op jit(solution)/shard_map/while/body/eval_jaxpr/ppermute | solution.py:14
  357.4 5.6 %convolution_convert_fusion.3 = bf16[197,3072]{1,0:T(8,128)(2,1)} fusion(bf16[1024,3072]{1,0:T(8,128)(2,1)} %get-tuple-element.539, f32[1024]{0:T(1024)} %bitcast.303, f32[197]{0:T(256)S(1)} %add_rsqrt_fusion.8, f32[197]{0:T(256)S(1)} %broadcast_multiply_fusion.10, f32[1,197,1024]{2,0,1:T(1,128)S(1)} %get-tuple-element.516, ...), kind=kOutput, calls=%fused_computation.2.clone.1 | convolution fusion | flops 1241232384 | bytes 8724524 | tf_op jit(solution)/shard_map/while/body/eval_jaxpr/gpd,de->gpe/dot_general | solution.py:30
  371.6 14.2 %fusion.344 = f32[1,197,1024]{2,1,0:T(8,128)S(1)} fusion(f32[1,197,1024]{2,1,0:T(8,128)S(1)} %get-tuple-element.495, bf16[4096,1024]{1,0:T(8,128)(2,1)} %get-tuple-element.543, bf16[1024,4096]{1,0:T(8,128)(2,1)} %get-tuple-element.542, f32[1024]{0:T(1024)S(1)} %bitcast.305, f32[197]{0:T(256)S(1)} %add_rsqrt_fusion.9, ...), kind=kOutput, calls=%fused_computation.61.clone.1 | convolution fusion | flops 3358569472 | bytes 18396712 | tf_op jit(solution)/shard_map/while/body/eval_jaxpr/gpf,fd->gpd/dot_general | solution.py:50
  386.6 4.4 collective-permute-start
  391.1 14.0 %collective-permute-done = f32[1,197,1024]{2,0,1:T(1,128)S(1)} collective-permute-done((f32[1,197,1024]{2,0,1:T(1,128)S(1)}, f32[1,197,1024]{2,0,1:T(1,128)S(1)}, u32[]{:S(2)}, u32[]{:S(2)}) %collective-permute-start) | collective-permute-done | bytes 806944 | tf_op jit(solution)/shard_map/while/body/eval_jaxpr/ppermute | solution.py:14
  410.4 3.8 convolution_convert_fusion.1
  414.2 4.6 collective-permute-start.8
  418.8 2.9 collective-permute-start.7
  423.6 3.6 collective-permute-start.5
  427.2 7.2 %collective-permute-start.4 = (bf16[3,2048]{1,0:T(4,128)(2,1)S(1)}, bf16[3,2048]{1,0:T(4,128)(2,1)S(1)}, u32[]{:S(2)}, u32[]{:S(2)}) collective-permute-start(bf16[3,2048]{1,0:T(4,128)(2,1)S(1)} %slice.122), channel_id=1, source_target_pairs={{2,0},{3,1},{4,2},{5,3},{6,4},{7,5},{8,6},{9,7},{10,8},{11,9},{12,... | collective-permute-start | bytes 36872 | tf_op jit(solution)/shard_map/ppermute | solution.py:14
  443.3 3.1 collective-permute-done.1
  452.4 8.1 %convolution_add_fusion = f32[3,1024]{1,0:T(4,128)S(1)} fusion(f32[3,1024]{1,0:T(4,128)S(1)} %get-tuple-element.399, f32[1024]{0:T(1024)S(1)} %bitcast.306, f32[3]{0:T(128)S(1)} %add_rsqrt_fusion.3, f32[3]{0:T(128)S(1)} %broadcast_multiply_fusion.4, bf16[1,4096,1024]{2,1,0:T(8,128)(2,1)} %bitcast.298, bf16[1,1024,4096]{2,1,0:T(8,128)(2,1)} %bitcast.296), kind=kOutput, calls=%fused_computation.161 | convolution fusion | flops 51145728 | bytes 16805912 | tf_op jit(solution)/shard_map/dot_general | solution.py:166
  460.5 10.4 %all_to_all.5 = f32[3,4,256]{2,0,1:T(4,128)S(1)} all-to-all(f32[3,4,256]{2,0,1:T(4,128)S(1)} %bitcast.302), channel_id=1, replica_groups=mesh['segment'=4,'lane'=32] {'segment'}, dimensions={1} | all-to-all | bytes 24576 | tf_op jit(solution)/shard_map/all_to_all | solution.py:168
  (258 shorter events, 100.9 us)
Async XLA Ops:
  6.5 64.8 %all-gather.5.cloned.1.call-start = ((), (), s32[]{:S(2)}) async-start(), calls=%async_computation.1 | async-start | bytes 8650752 | tf_op jit(solution)/shard_map/all_gather | solution.py:100
  7.3 119.3 %all-gather.7.cloned.1.call-start = ((), (), s32[]{:S(2)}) async-start(), calls=%async_computation.2 | async-start | bytes 8650752 | tf_op jit(solution)/shard_map/all_gather | solution.py:101
  143.7 39.3 %copy-start.2 = (f32[1024]{0:T(1024)S(1)}, f32[1024]{0:T(1024)}, u32[]{:S(2)}) copy-start(f32[1024]{0:T(1024)} %get-tuple-element.544) | copy-start | bytes 12292 | tf_op jit(solution)/shard_map/while
  158.8 21.1 %collective-permute-start = (f32[1,197,1024]{2,0,1:T(1,128)S(1)}, f32[1,197,1024]{2,0,1:T(1,128)S(1)}, u32[]{:S(2)}, u32[]{:S(2)}) collective-permute-start(f32[1,197,1024]{2,0,1:T(1,128)S(1)} %copy.298), channel_id=1, source_target_pairs={{0,32},{32,64},{64,96},{1,33},{33,65},{65,97},{2,34},{34,66},{66,9... | collective-permute-start | bytes 2420744 | tf_op jit(solution)/shard_map/while/body/eval_jaxpr/ppermute | solution.py:14
  198.1 3.1 copy-start.3
  201.2 39.5 %copy-start.2 = (f32[1024]{0:T(1024)S(1)}, f32[1024]{0:T(1024)}, u32[]{:S(2)}) copy-start(f32[1024]{0:T(1024)} %get-tuple-element.544) | copy-start | bytes 12292 | tf_op jit(solution)/shard_map/while
  216.3 21.2 %collective-permute-start = (f32[1,197,1024]{2,0,1:T(1,128)S(1)}, f32[1,197,1024]{2,0,1:T(1,128)S(1)}, u32[]{:S(2)}, u32[]{:S(2)}) collective-permute-start(f32[1,197,1024]{2,0,1:T(1,128)S(1)} %copy.298), channel_id=1, source_target_pairs={{0,32},{32,64},{64,96},{1,33},{33,65},{65,97},{2,34},{34,66},{66,9... | collective-permute-start | bytes 2420744 | tf_op jit(solution)/shard_map/while/body/eval_jaxpr/ppermute | solution.py:14
  258.9 38.6 %copy-start.2 = (f32[1024]{0:T(1024)S(1)}, f32[1024]{0:T(1024)}, u32[]{:S(2)}) copy-start(f32[1024]{0:T(1024)} %get-tuple-element.544) | copy-start | bytes 12292 | tf_op jit(solution)/shard_map/while
  274.0 20.3 %collective-permute-start = (f32[1,197,1024]{2,0,1:T(1,128)S(1)}, f32[1,197,1024]{2,0,1:T(1,128)S(1)}, u32[]{:S(2)}, u32[]{:S(2)}) collective-permute-start(f32[1,197,1024]{2,0,1:T(1,128)S(1)} %copy.298), channel_id=1, source_target_pairs={{0,32},{32,64},{64,96},{1,33},{33,65},{65,97},{2,34},{34,66},{66,9... | collective-permute-start | bytes 2420744 | tf_op jit(solution)/shard_map/while/body/eval_jaxpr/ppermute | solution.py:14
  315.7 37.7 %copy-start.2 = (f32[1024]{0:T(1024)S(1)}, f32[1024]{0:T(1024)}, u32[]{:S(2)}) copy-start(f32[1024]{0:T(1024)} %get-tuple-element.544) | copy-start | bytes 12292 | tf_op jit(solution)/shard_map/while
  330.8 19.4 %collective-permute-start = (f32[1,197,1024]{2,0,1:T(1,128)S(1)}, f32[1,197,1024]{2,0,1:T(1,128)S(1)}, u32[]{:S(2)}, u32[]{:S(2)}) collective-permute-start(f32[1,197,1024]{2,0,1:T(1,128)S(1)} %copy.298), channel_id=1, source_target_pairs={{0,32},{32,64},{64,96},{1,33},{33,65},{65,97},{2,34},{34,66},{66,9... | collective-permute-start | bytes 2420744 | tf_op jit(solution)/shard_map/while/body/eval_jaxpr/ppermute | solution.py:14
  371.6 36.8 %copy-start.2 = (f32[1024]{0:T(1024)S(1)}, f32[1024]{0:T(1024)}, u32[]{:S(2)}) copy-start(f32[1024]{0:T(1024)} %get-tuple-element.544) | copy-start | bytes 12292 | tf_op jit(solution)/shard_map/while
  386.6 18.5 %collective-permute-start = (f32[1,197,1024]{2,0,1:T(1,128)S(1)}, f32[1,197,1024]{2,0,1:T(1,128)S(1)}, u32[]{:S(2)}, u32[]{:S(2)}) collective-permute-start(f32[1,197,1024]{2,0,1:T(1,128)S(1)} %copy.298), channel_id=1, source_target_pairs={{0,32},{32,64},{64,96},{1,33},{33,65},{65,97},{2,34},{34,66},{66,9... | collective-permute-start | bytes 2420744 | tf_op jit(solution)/shard_map/while/body/eval_jaxpr/ppermute | solution.py:14
  409.9 24.7 %copy-start.13 = (pred[3,3]{0,1:T(4,128)(4,1)S(1)}, pred[3,3]{0,1:T(4,128)(4,1)}, u32[]{:S(2)}) copy-start(pred[3,3]{0,1:T(4,128)(4,1)} %get-tuple-element.379) | copy-start | bytes 31
  410.3 36.9 %copy-start.5 = (pred[3,3]{0,1:T(4,128)(4,1)S(1)}, pred[3,3]{0,1:T(4,128)(4,1)}, u32[]{:S(2)}) copy-start(pred[3,3]{0,1:T(4,128)(4,1)} %get-tuple-element.377) | copy-start | bytes 31
  410.3 37.1 %copy-start.6 = (pred[3,3]{0,1:T(4,128)(4,1)S(1)}, pred[3,3]{0,1:T(4,128)(4,1)}, u32[]{:S(2)}) copy-start(pred[3,3]{0,1:T(4,128)(4,1)} %get-tuple-element.376) | copy-start | bytes 31
  410.3 37.2 %copy-start.7 = (pred[3,3]{0,1:T(4,128)(4,1)S(1)}, pred[3,3]{0,1:T(4,128)(4,1)}, u32[]{:S(2)}) copy-start(pred[3,3]{0,1:T(4,128)(4,1)} %get-tuple-element.375) | copy-start | bytes 31
  410.3 37.4 %copy-start.8 = (pred[3,3]{0,1:T(4,128)(4,1)S(1)}, pred[3,3]{0,1:T(4,128)(4,1)}, u32[]{:S(2)}) copy-start(pred[3,3]{0,1:T(4,128)(4,1)} %get-tuple-element.374) | copy-start | bytes 31
  410.3 37.6 %copy-start.9 = (pred[3,3]{0,1:T(4,128)(4,1)S(1)}, pred[3,3]{0,1:T(4,128)(4,1)}, u32[]{:S(2)}) copy-start(pred[3,3]{0,1:T(4,128)(4,1)} %get-tuple-element.373) | copy-start | bytes 31
  410.3 37.7 %copy-start.10 = (pred[3,3]{0,1:T(4,128)(4,1)S(1)}, pred[3,3]{0,1:T(4,128)(4,1)}, u32[]{:S(2)}) copy-start(pred[3,3]{0,1:T(4,128)(4,1)} %get-tuple-element.372) | copy-start | bytes 31
  410.3 37.9 %copy-start.11 = (pred[3,3]{0,1:T(4,128)(4,1)S(1)}, pred[3,3]{0,1:T(4,128)(4,1)}, u32[]{:S(2)}) copy-start(pred[3,3]{0,1:T(4,128)(4,1)} %get-tuple-element.371) | copy-start | bytes 31
  410.3 38.0 %copy-start.12 = (pred[3,3]{0,1:T(4,128)(4,1)S(1)}, pred[3,3]{0,1:T(4,128)(4,1)}, u32[]{:S(2)}) copy-start(pred[3,3]{0,1:T(4,128)(4,1)} %get-tuple-element.378) | copy-start | bytes 31
  414.1 37.5 %copy-start.1 = (bf16[1024,1024]{1,0:T(8,128)(2,1)S(1)}, bf16[1024,1024]{1,0:T(8,128)(2,1)}, u32[]{:S(2)}) copy-start(bf16[1024,1024]{1,0:T(8,128)(2,1)} %get-tuple-element.554) | copy-start | bytes 6291460
  414.2 20.8 %collective-permute-start.8 = (bf16[3,2048]{1,0:T(4,128)(2,1)S(1)}, bf16[3,2048]{1,0:T(4,128)(2,1)S(1)}, u32[]{:S(2)}, u32[]{:S(2)}) collective-permute-start(bf16[3,2048]{1,0:T(4,128)(2,1)S(1)} %slice.122), channel_id=1, source_target_pairs={{4,0},{5,1},{6,2},{7,3},{8,4},{9,5},{10,6},{11,7},{12,8},{13,9},{1... | collective-permute-start | bytes 36872 | tf_op jit(solution)/shard_map/ppermute | solution.py:14
  418.8 18.1 %collective-permute-start.7 = (bf16[3,2048]{1,0:T(4,128)(2,1)S(1)}, bf16[3,2048]{1,0:T(4,128)(2,1)S(1)}, u32[]{:S(2)}, u32[]{:S(2)}) collective-permute-start(bf16[3,2048]{1,0:T(4,128)(2,1)S(1)} %slice.122), channel_id=1, source_target_pairs={{0,4},{1,5},{2,6},{3,7},{4,8},{5,9},{6,10},{7,11},{8,12},{9,13},{1... | collective-permute-start | bytes 36872 | tf_op jit(solution)/shard_map/ppermute | solution.py:14
  421.7 17.4 %collective-permute-start.6 = (bf16[3,2048]{1,0:T(4,128)(2,1)S(1)}, bf16[3,2048]{1,0:T(4,128)(2,1)S(1)}, u32[]{:S(2)}, u32[]{:S(2)}) collective-permute-start(bf16[3,2048]{1,0:T(4,128)(2,1)S(1)} %slice.122), channel_id=1, source_target_pairs={{3,0},{4,1},{5,2},{6,3},{7,4},{8,5},{9,6},{10,7},{11,8},{12,9},{13... | collective-permute-start | bytes 36872 | tf_op jit(solution)/shard_map/ppermute | solution.py:14
  423.6 17.7 %collective-permute-start.5 = (bf16[3,2048]{1,0:T(4,128)(2,1)S(1)}, bf16[3,2048]{1,0:T(4,128)(2,1)S(1)}, u32[]{:S(2)}, u32[]{:S(2)}) collective-permute-start(bf16[3,2048]{1,0:T(4,128)(2,1)S(1)} %slice.122), channel_id=1, source_target_pairs={{0,3},{1,4},{2,5},{3,6},{4,7},{5,8},{6,9},{7,10},{8,11},{9,12},{10... | collective-permute-start | bytes 36872 | tf_op jit(solution)/shard_map/ppermute | solution.py:14
  427.2 14.0 %collective-permute-start.4 = (bf16[3,2048]{1,0:T(4,128)(2,1)S(1)}, bf16[3,2048]{1,0:T(4,128)(2,1)S(1)}, u32[]{:S(2)}, u32[]{:S(2)}) collective-permute-start(bf16[3,2048]{1,0:T(4,128)(2,1)S(1)} %slice.122), channel_id=1, source_target_pairs={{2,0},{3,1},{4,2},{5,3},{6,4},{7,5},{8,6},{9,7},{10,8},{11,9},{12,... | collective-permute-start | bytes 36872 | tf_op jit(solution)/shard_map/ppermute | solution.py:14
  434.9 7.7 %collective-permute-start.3 = (bf16[3,2048]{1,0:T(4,128)(2,1)S(1)}, bf16[3,2048]{1,0:T(4,128)(2,1)S(1)}, u32[]{:S(2)}, u32[]{:S(2)}) collective-permute-start(bf16[3,2048]{1,0:T(4,128)(2,1)S(1)} %slice.122), channel_id=1, source_target_pairs={{0,2},{1,3},{2,4},{3,5},{4,6},{5,7},{6,8},{7,9},{8,10},{9,11},{10,... | collective-permute-start | bytes 36872 | tf_op jit(solution)/shard_map/ppermute | solution.py:14
  436.9 5.8 %collective-permute-start.2 = (bf16[3,2048]{1,0:T(4,128)(2,1)S(1)}, bf16[3,2048]{1,0:T(4,128)(2,1)S(1)}, u32[]{:S(2)}, u32[]{:S(2)}) collective-permute-start(bf16[3,2048]{1,0:T(4,128)(2,1)S(1)} %slice.122), channel_id=1, source_target_pairs={{1,0},{2,1},{3,2},{4,3},{5,4},{6,5},{7,6},{8,7},{9,8},{10,9},{11,1... | collective-permute-start | bytes 36872 | tf_op jit(solution)/shard_map/ppermute | solution.py:14
  439.1 7.3 %collective-permute-start.1 = (bf16[3,2048]{1,0:T(4,128)(2,1)S(1)}, bf16[3,2048]{1,0:T(4,128)(2,1)S(1)}, u32[]{:S(2)}, u32[]{:S(2)}) collective-permute-start(bf16[3,2048]{1,0:T(4,128)(2,1)S(1)} %slice.122), channel_id=1, source_target_pairs={{0,1},{1,2},{2,3},{3,4},{4,5},{5,6},{6,7},{7,8},{8,9},{9,10},{10,1... | collective-permute-start | bytes 36872 | tf_op jit(solution)/shard_map/ppermute | solution.py:14
  446.8 5.5 %copy-start.4 = (f32[1,1024]{1,0:T(1,128)S(1)}, f32[1,1024]{1,0:T(1,128)}, u32[]{:S(2)}) copy-start(f32[1,1024]{1,0:T(1,128)} %get-tuple-element.582) | copy-start | bytes 12292
  (9 other events, 20.5 us)
Sparse Core Ops, SparseCore 0:
  9.5 61.7 all-gather.4
  73.6 52.9 all-gather.6
where the time goes:
time: 480 us; the launch traced here: 478 us
  waiting for transfers between devices  201 us (42%)
  matrix products  129 us (27%)
  other arithmetic  52.1 us (11%)
  starting transfers between devices  47.8 us (10%)
  local copies, waits for them, and re-layouts  22 us (5%)
  between operations  14.1 us (3%)
  blocking collectives  10.4 us (2%)
    ppermute x13, waiting for transfers between devices, from_behind(): lax.ppermute(value, axis, [(source, source + steps) for source in range(l...  83.6 us
    dot_general x5, matrix products, spatial_layer(): jnp.einsum('gpf,fd->gpd', hidden, reduce_weight, preferred_element_type=j...  71.1 us
    all_gather x1, waiting for transfers between devices, body(): lax.all_gather(expand_weight[0], 'lane', axis=1, tiled=True)  61.2 us
    all_gather x1, waiting for transfers between devices, body(): lax.all_gather(reduce_weight[0], 'lane', axis=0, tiled=True)  55.2 us
    ppermute x13, starting transfers between devices, from_behind(): lax.ppermute(value, axis, [(source, source + steps) for source in range(l...  47.7 us
    dot_general x5, matrix products, spatial_layer(): jnp.einsum('gpd,de->gpe', normed, triple_weight, preferred_element_type=j...  28 us
    reduce_sum x17, other arithmetic, normalize(): spread = jnp.mean(centred * centred, axis=-1, keepdims=True)  18.5 us
    sub x5, other arithmetic, spatial_layer(): weights = jax.nn.softmax(scores, axis=-1).astype(jnp.bfloat16)  13.5 us
  transfers between devices with their start and end apart: 15, of which 9 were waited for; matrix products, arithmetic and copies ran while one was open for 1% of the time, Pallas kernels for 0%

commit v1 on v0

--- a/solution.py
+++ b/solution.py
@@ -165,7 +165,15 @@
     ).astype(jnp.bfloat16)
     temporal = temporal + jnp.dot(hidden, reduce_full, preferred_element_type=jnp.float32)
     columns = temporal.reshape(frame_count, segment_count, model_width // segment_count)
-    shared = lax.all_to_all(columns, "segment", split_axis=1, concat_axis=1, tiled=True)
+    shared = jnp.concatenate(
+        jax.lax.all_to_all(
+            jnp.stack(jnp.split(columns, jax.lax.axis_size("segment"), axis=1)),
+            axis_name="segment",
+            split_axis=0,
+            concat_axis=0,
+        ),
+        axis=1,
+    )
     return shared[:, segment_count - 1]
 
 

time: 480 us -> 480 us (level)
  no operation moved by 1% of the time
where the time goes in v1:
time: 480 us; the launch traced here: 478 us
  waiting for transfers between devices  201 us (42%)
  matrix products  129 us (27%)
  other arithmetic  52.2 us (11%)
  starting transfers between devices  47.8 us (10%)
  local copies, waits for them, and re-layouts  22.1 us (5%)
  between operations  14.1 us (3%)
  blocking collectives  10.4 us (2%)
    ppermute x13, waiting for transfers between devices, from_behind(): lax.ppermute(value, axis, [(source, source + steps) for source in range(l...  83.6 us
    dot_general x5, matrix products, spatial_layer(): jnp.einsum('gpf,fd->gpd', hidden, reduce_weight, preferred_element_type=j...  71.1 us
    all_gather x1, waiting for transfers between devices, body(): lax.all_gather(expand_weight[0], 'lane', axis=1, tiled=True)  61.2 us
    all_gather x1, waiting for transfers between devices, body(): lax.all_gather(reduce_weight[0], 'lane', axis=0, tiled=True)  55.2 us
    ppermute x13, starting transfers between devices, from_behind(): lax.ppermute(value, axis, [(source, source + steps) for source in range(l...  47.7 us
    dot_general x5, matrix products, spatial_layer(): jnp.einsum('gpd,de->gpe', normed, triple_weight, preferred_element_type=j...  28 us
    reduce_sum x17, other arithmetic, normalize(): spread = jnp.mean(centred * centred, axis=-1, keepdims=True)  18.5 us
    sub x5, other arithmetic, spatial_layer(): weights = jax.nn.softmax(scores, axis=-1).astype(jnp.bfloat16)  13.5 us
  transfers between devices with their start and end apart: 15, of which 9 were waited for; matrix products, arithmetic and copies ran while one was open for 1% of the time, Pallas kernels for 0%

profile of v1, /device:TPU:2, one launch (start us, length us, event | category | flops | bytes accessed | tf_op | source)
XLA Modules:
  0.0 478.4 jit_solution(15995879816722869848)
XLA Ops:
  10.1 61.2 %all-gather.5.cloned.1.call-done = bf16[1,1024,4096]{2,1,0:T(8,128)(2,1)} async-done(((bf16[1,1024,128]{2,1,0:T(8,128)(2,1)}), bf16[1,1024,4096]{2,1,0:T(8,128)(2,1)}) %all-gather.5.cloned.1.call-update) | async-done | bytes 8388624 | tf_op jit(solution)/shard_map/all_gather | solution.py:100
  71.3 55.2 %all-gather.7.cloned.1.call-done = bf16[1,4096,1024]{2,1,0:T(8,128)(2,1)} async-done(((bf16[1,128,1024]{2,1,0:T(8,128)(2,1)}), bf16[1,4096,1024]{2,1,0:T(8,128)(2,1)}) %all-gather.7.cloned.1.call-update) | async-done | bytes 8388624 | tf_op jit(solution)/shard_map/all_gather | solution.py:101
  127.0 283.0 %while.17 = (s32[]{:T(128)}, f32[1,197,1024]{2,0,1:T(1,128)S(1)}, f32[3,1024]{1,0:T(4,128)S(1)}, pred[]{:T(512)}, bf16[3,197,1024]{2,1,0:T(8,128)(2,1)}, /*index...) while((s32[]{:T(128)}, f32[1,197,1024]{2,0,1:T(1,128)S(1)}, ...), condition=%wide.region_10.11_spmd, body=%wide.region_0.10_spmd.sunk | while | flops 5180471808 | bytes 65759924 | solution.py:130
  129.5 5.6 %convolution_convert_fusion.3 = bf16[197,3072]{1,0:T(8,128)(2,1)} fusion(bf16[1024,3072]{1,0:T(8,128)(2,1)} %get-tuple-element.543, f32[1024]{0:T(1024)} %bitcast.316, f32[197]{0:T(256)S(1)} %add_rsqrt_fusion.8, f32[197]{0:T(256)S(1)} %broadcast_multiply_fusion.10, f32[1,197,1024]{2,0,1:T(1,128)S(1)} %get-tuple-element.520, ...), kind=kOutput, calls=%fused_computation.2.clone.1 | convolution fusion | flops 1241232384 | bytes 8724524 | tf_op jit(solution)/shard_map/while/body/eval_jaxpr/gpd,de->gpe/dot_general | solution.py:30
  137.4 2.7 fusion.341
  143.7 14.2 %fusion.344 = f32[1,197,1024]{2,1,0:T(8,128)S(1)} fusion(f32[1,197,1024]{2,1,0:T(8,128)S(1)} %get-tuple-element.499, bf16[4096,1024]{1,0:T(8,128)(2,1)} %get-tuple-element.547, bf16[1024,4096]{1,0:T(8,128)(2,1)} %get-tuple-element.546, f32[1024]{0:T(1024)S(1)} %bitcast.318, f32[197]{0:T(256)S(1)} %add_rsqrt_fusion.9, ...), kind=kOutput, calls=%fused_computation.61.clone.1 | convolution fusion | flops 3358569472 | bytes 18396712 | tf_op jit(solution)/shard_map/while/body/eval_jaxpr/gpf,fd->gpd/dot_general | solution.py:50
  158.8 3.4 collective-permute-start
  162.2 17.6 %collective-permute-done = f32[1,197,1024]{2,0,1:T(1,128)S(1)} collective-permute-done((f32[1,197,1024]{2,0,1:T(1,128)S(1)}, f32[1,197,1024]{2,0,1:T(1,128)S(1)}, u32[]{:S(2)}, u32[]{:S(2)}) %collective-permute-start) | collective-permute-done | bytes 806944 | tf_op jit(solution)/shard_map/while/body/eval_jaxpr/ppermute | solution.py:14
  187.0 5.6 %convolution_convert_fusion.3 = bf16[197,3072]{1,0:T(8,128)(2,1)} fusion(bf16[1024,3072]{1,0:T(8,128)(2,1)} %get-tuple-element.543, f32[1024]{0:T(1024)} %bitcast.316, f32[197]{0:T(256)S(1)} %add_rsqrt_fusion.8, f32[197]{0:T(256)S(1)} %broadcast_multiply_fusion.10, f32[1,197,1024]{2,0,1:T(1,128)S(1)} %get-tuple-element.520, ...), kind=kOutput, calls=%fused_computation.2.clone.1 | convolution fusion | flops 1241232384 | bytes 8724524 | tf_op jit(solution)/shard_map/while/body/eval_jaxpr/gpd,de->gpe/dot_general | solution.py:30
  201.2 14.2 %fusion.344 = f32[1,197,1024]{2,1,0:T(8,128)S(1)} fusion(f32[1,197,1024]{2,1,0:T(8,128)S(1)} %get-tuple-element.499, bf16[4096,1024]{1,0:T(8,128)(2,1)} %get-tuple-element.547, bf16[1024,4096]{1,0:T(8,128)(2,1)} %get-tuple-element.546, f32[1024]{0:T(1024)S(1)} %bitcast.318, f32[197]{0:T(256)S(1)} %add_rsqrt_fusion.9, ...), kind=kOutput, calls=%fused_computation.61.clone.1 | convolution fusion | flops 3358569472 | bytes 18396712 | tf_op jit(solution)/shard_map/while/body/eval_jaxpr/gpf,fd->gpd/dot_general | solution.py:50
  216.3 4.4 collective-permute-start
  220.7 16.8 %collective-permute-done = f32[1,197,1024]{2,0,1:T(1,128)S(1)} collective-permute-done((f32[1,197,1024]{2,0,1:T(1,128)S(1)}, f32[1,197,1024]{2,0,1:T(1,128)S(1)}, u32[]{:S(2)}, u32[]{:S(2)}) %collective-permute-start) | collective-permute-done | bytes 806944 | tf_op jit(solution)/shard_map/while/body/eval_jaxpr/ppermute | solution.py:14
  244.7 5.6 %convolution_convert_fusion.3 = bf16[197,3072]{1,0:T(8,128)(2,1)} fusion(bf16[1024,3072]{1,0:T(8,128)(2,1)} %get-tuple-element.543, f32[1024]{0:T(1024)} %bitcast.316, f32[197]{0:T(256)S(1)} %add_rsqrt_fusion.8, f32[197]{0:T(256)S(1)} %broadcast_multiply_fusion.10, f32[1,197,1024]{2,0,1:T(1,128)S(1)} %get-tuple-element.520, ...), kind=kOutput, calls=%fused_computation.2.clone.1 | convolution fusion | flops 1241232384 | bytes 8724524 | tf_op jit(solution)/shard_map/while/body/eval_jaxpr/gpd,de->gpe/dot_general | solution.py:30
  258.9 14.2 %fusion.344 = f32[1,197,1024]{2,1,0:T(8,128)S(1)} fusion(f32[1,197,1024]{2,1,0:T(8,128)S(1)} %get-tuple-element.499, bf16[4096,1024]{1,0:T(8,128)(2,1)} %get-tuple-element.547, bf16[1024,4096]{1,0:T(8,128)(2,1)} %get-tuple-element.546, f32[1024]{0:T(1024)S(1)} %bitcast.318, f32[197]{0:T(256)S(1)} %add_rsqrt_fusion.9, ...), kind=kOutput, calls=%fused_computation.61.clone.1 | convolution fusion | flops 3358569472 | bytes 18396712 | tf_op jit(solution)/shard_map/while/body/eval_jaxpr/gpf,fd->gpd/dot_general | solution.py:50
  274.0 4.4 collective-permute-start
  278.4 15.9 %collective-permute-done = f32[1,197,1024]{2,0,1:T(1,128)S(1)} collective-permute-done((f32[1,197,1024]{2,0,1:T(1,128)S(1)}, f32[1,197,1024]{2,0,1:T(1,128)S(1)}, u32[]{:S(2)}, u32[]{:S(2)}) %collective-permute-start) | collective-permute-done | bytes 806944 | tf_op jit(solution)/shard_map/while/body/eval_jaxpr/ppermute | solution.py:14
  301.5 5.6 %convolution_convert_fusion.3 = bf16[197,3072]{1,0:T(8,128)(2,1)} fusion(bf16[1024,3072]{1,0:T(8,128)(2,1)} %get-tuple-element.543, f32[1024]{0:T(1024)} %bitcast.316, f32[197]{0:T(256)S(1)} %add_rsqrt_fusion.8, f32[197]{0:T(256)S(1)} %broadcast_multiply_fusion.10, f32[1,197,1024]{2,0,1:T(1,128)S(1)} %get-tuple-element.520, ...), kind=kOutput, calls=%fused_computation.2.clone.1 | convolution fusion | flops 1241232384 | bytes 8724524 | tf_op jit(solution)/shard_map/while/body/eval_jaxpr/gpd,de->gpe/dot_general | solution.py:30
  315.7 14.2 %fusion.344 = f32[1,197,1024]{2,1,0:T(8,128)S(1)} fusion(f32[1,197,1024]{2,1,0:T(8,128)S(1)} %get-tuple-element.499, bf16[4096,1024]{1,0:T(8,128)(2,1)} %get-tuple-element.547, bf16[1024,4096]{1,0:T(8,128)(2,1)} %get-tuple-element.546, f32[1024]{0:T(1024)S(1)} %bitcast.318, f32[197]{0:T(256)S(1)} %add_rsqrt_fusion.9, ...), kind=kOutput, calls=%fused_computation.61.clone.1 | convolution fusion | flops 3358569472 | bytes 18396712 | tf_op jit(solution)/shard_map/while/body/eval_jaxpr/gpf,fd->gpd/dot_general | solution.py:50
  330.8 4.4 collective-permute-start
  335.2 14.9 %collective-permute-done = f32[1,197,1024]{2,0,1:T(1,128)S(1)} collective-permute-done((f32[1,197,1024]{2,0,1:T(1,128)S(1)}, f32[1,197,1024]{2,0,1:T(1,128)S(1)}, u32[]{:S(2)}, u32[]{:S(2)}) %collective-permute-start) | collective-permute-done | bytes 806944 | tf_op jit(solution)/shard_map/while/body/eval_jaxpr/ppermute | solution.py:14
  357.4 5.6 %convolution_convert_fusion.3 = bf16[197,3072]{1,0:T(8,128)(2,1)} fusion(bf16[1024,3072]{1,0:T(8,128)(2,1)} %get-tuple-element.543, f32[1024]{0:T(1024)} %bitcast.316, f32[197]{0:T(256)S(1)} %add_rsqrt_fusion.8, f32[197]{0:T(256)S(1)} %broadcast_multiply_fusion.10, f32[1,197,1024]{2,0,1:T(1,128)S(1)} %get-tuple-element.520, ...), kind=kOutput, calls=%fused_computation.2.clone.1 | convolution fusion | flops 1241232384 | bytes 8724524 | tf_op jit(solution)/shard_map/while/body/eval_jaxpr/gpd,de->gpe/dot_general | solution.py:30
  371.6 14.2 %fusion.344 = f32[1,197,1024]{2,1,0:T(8,128)S(1)} fusion(f32[1,197,1024]{2,1,0:T(8,128)S(1)} %get-tuple-element.499, bf16[4096,1024]{1,0:T(8,128)(2,1)} %get-tuple-element.547, bf16[1024,4096]{1,0:T(8,128)(2,1)} %get-tuple-element.546, f32[1024]{0:T(1024)S(1)} %bitcast.318, f32[197]{0:T(256)S(1)} %add_rsqrt_fusion.9, ...), kind=kOutput, calls=%fused_computation.61.clone.1 | convolution fusion | flops 3358569472 | bytes 18396712 | tf_op jit(solution)/shard_map/while/body/eval_jaxpr/gpf,fd->gpd/dot_general | solution.py:50
  386.6 4.4 collective-permute-start
  391.1 14.0 %collective-permute-done = f32[1,197,1024]{2,0,1:T(1,128)S(1)} collective-permute-done((f32[1,197,1024]{2,0,1:T(1,128)S(1)}, f32[1,197,1024]{2,0,1:T(1,128)S(1)}, u32[]{:S(2)}, u32[]{:S(2)}) %collective-permute-start) | collective-permute-done | bytes 806944 | tf_op jit(solution)/shard_map/while/body/eval_jaxpr/ppermute | solution.py:14
  410.4 3.8 convolution_convert_fusion.1
  414.2 4.6 collective-permute-start.8
  418.8 2.9 collective-permute-start.7
  423.6 3.6 collective-permute-start.5
  427.2 7.2 %collective-permute-start.4 = (bf16[3,2048]{1,0:T(4,128)(2,1)S(1)}, bf16[3,2048]{1,0:T(4,128)(2,1)S(1)}, u32[]{:S(2)}, u32[]{:S(2)}) collective-permute-start(bf16[3,2048]{1,0:T(4,128)(2,1)S(1)} %slice.122), channel_id=1, source_target_pairs={{2,0},{3,1},{4,2},{5,3},{6,4},{7,5},{8,6},{9,7},{10,8},{11,9},{12,... | collective-permute-start | bytes 36872 | tf_op jit(solution)/shard_map/ppermute | solution.py:14
  443.3 3.1 collective-permute-done.1
  452.4 8.1 %convolution_add_fusion = f32[3,1024]{1,0:T(4,128)S(1)} fusion(f32[3,1024]{1,0:T(4,128)S(1)} %get-tuple-element.403, f32[1024]{0:T(1024)S(1)} %bitcast.319, f32[3]{0:T(128)S(1)} %add_rsqrt_fusion.3, f32[3]{0:T(128)S(1)} %broadcast_multiply_fusion.4, bf16[1,4096,1024]{2,1,0:T(8,128)(2,1)} %bitcast.310, bf16[1,1024,4096]{2,1,0:T(8,128)(2,1)} %bitcast.308), kind=kOutput, calls=%fused_computation.161 | convolution fusion | flops 51145728 | bytes 16805912 | tf_op jit(solution)/shard_map/dot_general | solution.py:166
  460.5 10.4 %all_to_all.5 = f32[4,3,1,256]{3,2,1,0:T(1,128)S(1)} all-to-all(f32[4,3,1,256]{3,2,1,0:T(1,128)S(1)} %pad_maximum_fusion), channel_id=1, replica_groups=mesh['segment'=4,'lane'=32] {'segment'}, dimensions={0} | all-to-all | bytes 24576 | tf_op jit(solution)/shard_map/all_to_all | solution.py:169
  (263 shorter events, 101.0 us)
Async XLA Ops:
  6.5 64.8 %all-gather.5.cloned.1.call-start = ((), (), s32[]{:S(2)}) async-start(), calls=%async_computation.1 | async-start | bytes 8650752 | tf_op jit(solution)/shard_map/all_gather | solution.py:100
  7.3 119.3 %all-gather.7.cloned.1.call-start = ((), (), s32[]{:S(2)}) async-start(), calls=%async_computation.2 | async-start | bytes 8650752 | tf_op jit(solution)/shard_map/all_gather | solution.py:101
  143.7 39.3 %copy-start.2 = (f32[1024]{0:T(1024)S(1)}, f32[1024]{0:T(1024)}, u32[]{:S(2)}) copy-start(f32[1024]{0:T(1024)} %get-tuple-element.548) | copy-start | bytes 12292 | tf_op jit(solution)/shard_map/while
  158.8 21.1 %collective-permute-start = (f32[1,197,1024]{2,0,1:T(1,128)S(1)}, f32[1,197,1024]{2,0,1:T(1,128)S(1)}, u32[]{:S(2)}, u32[]{:S(2)}) collective-permute-start(f32[1,197,1024]{2,0,1:T(1,128)S(1)} %copy.351), channel_id=1, source_target_pairs={{0,32},{32,64},{64,96},{1,33},{33,65},{65,97},{2,34},{34,66},{66,9... | collective-permute-start | bytes 2420744 | tf_op jit(solution)/shard_map/while/body/eval_jaxpr/ppermute | solution.py:14
  198.1 3.1 copy-start.3
  201.2 39.5 %copy-start.2 = (f32[1024]{0:T(1024)S(1)}, f32[1024]{0:T(1024)}, u32[]{:S(2)}) copy-start(f32[1024]{0:T(1024)} %get-tuple-element.548) | copy-start | bytes 12292 | tf_op jit(solution)/shard_map/while
  216.3 21.2 %collective-permute-start = (f32[1,197,1024]{2,0,1:T(1,128)S(1)}, f32[1,197,1024]{2,0,1:T(1,128)S(1)}, u32[]{:S(2)}, u32[]{:S(2)}) collective-permute-start(f32[1,197,1024]{2,0,1:T(1,128)S(1)} %copy.351), channel_id=1, source_target_pairs={{0,32},{32,64},{64,96},{1,33},{33,65},{65,97},{2,34},{34,66},{66,9... | collective-permute-start | bytes 2420744 | tf_op jit(solution)/shard_map/while/body/eval_jaxpr/ppermute | solution.py:14
  258.9 38.6 %copy-start.2 = (f32[1024]{0:T(1024)S(1)}, f32[1024]{0:T(1024)}, u32[]{:S(2)}) copy-start(f32[1024]{0:T(1024)} %get-tuple-element.548) | copy-start | bytes 12292 | tf_op jit(solution)/shard_map/while
  274.0 20.3 %collective-permute-start = (f32[1,197,1024]{2,0,1:T(1,128)S(1)}, f32[1,197,1024]{2,0,1:T(1,128)S(1)}, u32[]{:S(2)}, u32[]{:S(2)}) collective-permute-start(f32[1,197,1024]{2,0,1:T(1,128)S(1)} %copy.351), channel_id=1, source_target_pairs={{0,32},{32,64},{64,96},{1,33},{33,65},{65,97},{2,34},{34,66},{66,9... | collective-permute-start | bytes 2420744 | tf_op jit(solution)/shard_map/while/body/eval_jaxpr/ppermute | solution.py:14
  315.7 37.7 %copy-start.2 = (f32[1024]{0:T(1024)S(1)}, f32[1024]{0:T(1024)}, u32[]{:S(2)}) copy-start(f32[1024]{0:T(1024)} %get-tuple-element.548) | copy-start | bytes 12292 | tf_op jit(solution)/shard_map/while
  330.8 19.4 %collective-permute-start = (f32[1,197,1024]{2,0,1:T(1,128)S(1)}, f32[1,197,1024]{2,0,1:T(1,128)S(1)}, u32[]{:S(2)}, u32[]{:S(2)}) collective-permute-start(f32[1,197,1024]{2,0,1:T(1,128)S(1)} %copy.351), channel_id=1, source_target_pairs={{0,32},{32,64},{64,96},{1,33},{33,65},{65,97},{2,34},{34,66},{66,9... | collective-permute-start | bytes 2420744 | tf_op jit(solution)/shard_map/while/body/eval_jaxpr/ppermute | solution.py:14
  371.6 36.8 %copy-start.2 = (f32[1024]{0:T(1024)S(1)}, f32[1024]{0:T(1024)}, u32[]{:S(2)}) copy-start(f32[1024]{0:T(1024)} %get-tuple-element.548) | copy-start | bytes 12292 | tf_op jit(solution)/shard_map/while
  386.6 18.5 %collective-permute-start = (f32[1,197,1024]{2,0,1:T(1,128)S(1)}, f32[1,197,1024]{2,0,1:T(1,128)S(1)}, u32[]{:S(2)}, u32[]{:S(2)}) collective-permute-start(f32[1,197,1024]{2,0,1:T(1,128)S(1)} %copy.351), channel_id=1, source_target_pairs={{0,32},{32,64},{64,96},{1,33},{33,65},{65,97},{2,34},{34,66},{66,9... | collective-permute-start | bytes 2420744 | tf_op jit(solution)/shard_map/while/body/eval_jaxpr/ppermute | solution.py:14
  409.9 24.7 %copy-start.13 = (pred[3,3]{0,1:T(4,128)(4,1)S(1)}, pred[3,3]{0,1:T(4,128)(4,1)}, u32[]{:S(2)}) copy-start(pred[3,3]{0,1:T(4,128)(4,1)} %get-tuple-element.383) | copy-start | bytes 31
  410.3 36.9 %copy-start.5 = (pred[3,3]{0,1:T(4,128)(4,1)S(1)}, pred[3,3]{0,1:T(4,128)(4,1)}, u32[]{:S(2)}) copy-start(pred[3,3]{0,1:T(4,128)(4,1)} %get-tuple-element.381) | copy-start | bytes 31
  410.3 37.1 %copy-start.6 = (pred[3,3]{0,1:T(4,128)(4,1)S(1)}, pred[3,3]{0,1:T(4,128)(4,1)}, u32[]{:S(2)}) copy-start(pred[3,3]{0,1:T(4,128)(4,1)} %get-tuple-element.380) | copy-start | bytes 31
  410.3 37.2 %copy-start.7 = (pred[3,3]{0,1:T(4,128)(4,1)S(1)}, pred[3,3]{0,1:T(4,128)(4,1)}, u32[]{:S(2)}) copy-start(pred[3,3]{0,1:T(4,128)(4,1)} %get-tuple-element.379) | copy-start | bytes 31
  410.3 37.4 %copy-start.8 = (pred[3,3]{0,1:T(4,128)(4,1)S(1)}, pred[3,3]{0,1:T(4,128)(4,1)}, u32[]{:S(2)}) copy-start(pred[3,3]{0,1:T(4,128)(4,1)} %get-tuple-element.378) | copy-start | bytes 31
  410.3 37.6 %copy-start.9 = (pred[3,3]{0,1:T(4,128)(4,1)S(1)}, pred[3,3]{0,1:T(4,128)(4,1)}, u32[]{:S(2)}) copy-start(pred[3,3]{0,1:T(4,128)(4,1)} %get-tuple-element.377) | copy-start | bytes 31
  410.3 37.7 %copy-start.10 = (pred[3,3]{0,1:T(4,128)(4,1)S(1)}, pred[3,3]{0,1:T(4,128)(4,1)}, u32[]{:S(2)}) copy-start(pred[3,3]{0,1:T(4,128)(4,1)} %get-tuple-element.376) | copy-start | bytes 31
  410.3 37.9 %copy-start.11 = (pred[3,3]{0,1:T(4,128)(4,1)S(1)}, pred[3,3]{0,1:T(4,128)(4,1)}, u32[]{:S(2)}) copy-start(pred[3,3]{0,1:T(4,128)(4,1)} %get-tuple-element.375) | copy-start | bytes 31
  410.3 38.0 %copy-start.12 = (pred[3,3]{0,1:T(4,128)(4,1)S(1)}, pred[3,3]{0,1:T(4,128)(4,1)}, u32[]{:S(2)}) copy-start(pred[3,3]{0,1:T(4,128)(4,1)} %get-tuple-element.382) | copy-start | bytes 31
  414.1 37.5 %copy-start.1 = (bf16[1024,1024]{1,0:T(8,128)(2,1)S(1)}, bf16[1024,1024]{1,0:T(8,128)(2,1)}, u32[]{:S(2)}) copy-start(bf16[1024,1024]{1,0:T(8,128)(2,1)} %get-tuple-element.558) | copy-start | bytes 6291460
  414.2 20.8 %collective-permute-start.8 = (bf16[3,2048]{1,0:T(4,128)(2,1)S(1)}, bf16[3,2048]{1,0:T(4,128)(2,1)S(1)}, u32[]{:S(2)}, u32[]{:S(2)}) collective-permute-start(bf16[3,2048]{1,0:T(4,128)(2,1)S(1)} %slice.122), channel_id=1, source_target_pairs={{4,0},{5,1},{6,2},{7,3},{8,4},{9,5},{10,6},{11,7},{12,8},{13,9},{1... | collective-permute-start | bytes 36872 | tf_op jit(solution)/shard_map/ppermute | solution.py:14
  418.8 18.1 %collective-permute-start.7 = (bf16[3,2048]{1,0:T(4,128)(2,1)S(1)}, bf16[3,2048]{1,0:T(4,128)(2,1)S(1)}, u32[]{:S(2)}, u32[]{:S(2)}) collective-permute-start(bf16[3,2048]{1,0:T(4,128)(2,1)S(1)} %slice.122), channel_id=1, source_target_pairs={{0,4},{1,5},{2,6},{3,7},{4,8},{5,9},{6,10},{7,11},{8,12},{9,13},{1... | collective-permute-start | bytes 36872 | tf_op jit(solution)/shard_map/ppermute | solution.py:14
  421.7 17.4 %collective-permute-start.6 = (bf16[3,2048]{1,0:T(4,128)(2,1)S(1)}, bf16[3,2048]{1,0:T(4,128)(2,1)S(1)}, u32[]{:S(2)}, u32[]{:S(2)}) collective-permute-start(bf16[3,2048]{1,0:T(4,128)(2,1)S(1)} %slice.122), channel_id=1, source_target_pairs={{3,0},{4,1},{5,2},{6,3},{7,4},{8,5},{9,6},{10,7},{11,8},{12,9},{13... | collective-permute-start | bytes 36872 | tf_op jit(solution)/shard_map/ppermute | solution.py:14
  423.6 17.7 %collective-permute-start.5 = (bf16[3,2048]{1,0:T(4,128)(2,1)S(1)}, bf16[3,2048]{1,0:T(4,128)(2,1)S(1)}, u32[]{:S(2)}, u32[]{:S(2)}) collective-permute-start(bf16[3,2048]{1,0:T(4,128)(2,1)S(1)} %slice.122), channel_id=1, source_target_pairs={{0,3},{1,4},{2,5},{3,6},{4,7},{5,8},{6,9},{7,10},{8,11},{9,12},{10... | collective-permute-start | bytes 36872 | tf_op jit(solution)/shard_map/ppermute | solution.py:14
  427.2 14.0 %collective-permute-start.4 = (bf16[3,2048]{1,0:T(4,128)(2,1)S(1)}, bf16[3,2048]{1,0:T(4,128)(2,1)S(1)}, u32[]{:S(2)}, u32[]{:S(2)}) collective-permute-start(bf16[3,2048]{1,0:T(4,128)(2,1)S(1)} %slice.122), channel_id=1, source_target_pairs={{2,0},{3,1},{4,2},{5,3},{6,4},{7,5},{8,6},{9,7},{10,8},{11,9},{12,... | collective-permute-start | bytes 36872 | tf_op jit(solution)/shard_map/ppermute | solution.py:14
  434.9 7.7 %collective-permute-start.3 = (bf16[3,2048]{1,0:T(4,128)(2,1)S(1)}, bf16[3,2048]{1,0:T(4,128)(2,1)S(1)}, u32[]{:S(2)}, u32[]{:S(2)}) collective-permute-start(bf16[3,2048]{1,0:T(4,128)(2,1)S(1)} %slice.122), channel_id=1, source_target_pairs={{0,2},{1,3},{2,4},{3,5},{4,6},{5,7},{6,8},{7,9},{8,10},{9,11},{10,... | collective-permute-start | bytes 36872 | tf_op jit(solution)/shard_map/ppermute | solution.py:14
  436.9 5.8 %collective-permute-start.2 = (bf16[3,2048]{1,0:T(4,128)(2,1)S(1)}, bf16[3,2048]{1,0:T(4,128)(2,1)S(1)}, u32[]{:S(2)}, u32[]{:S(2)}) collective-permute-start(bf16[3,2048]{1,0:T(4,128)(2,1)S(1)} %slice.122), channel_id=1, source_target_pairs={{1,0},{2,1},{3,2},{4,3},{5,4},{6,5},{7,6},{8,7},{9,8},{10,9},{11,1... | collective-permute-start | bytes 36872 | tf_op jit(solution)/shard_map/ppermute | solution.py:14
  439.1 7.3 %collective-permute-start.1 = (bf16[3,2048]{1,0:T(4,128)(2,1)S(1)}, bf16[3,2048]{1,0:T(4,128)(2,1)S(1)}, u32[]{:S(2)}, u32[]{:S(2)}) collective-permute-start(bf16[3,2048]{1,0:T(4,128)(2,1)S(1)} %slice.122), channel_id=1, source_target_pairs={{0,1},{1,2},{2,3},{3,4},{4,5},{5,6},{6,7},{7,8},{8,9},{9,10},{10,1... | collective-permute-start | bytes 36872 | tf_op jit(solution)/shard_map/ppermute | solution.py:14
  446.8 5.5 %copy-start.4 = (f32[1,1024]{1,0:T(1,128)S(1)}, f32[1,1024]{1,0:T(1,128)}, u32[]{:S(2)}) copy-start(f32[1,1024]{1,0:T(1,128)} %get-tuple-element.586) | copy-start | bytes 12292
  (9 other events, 20.5 us)
Sparse Core Ops, SparseCore 0:
  9.5 61.7 all-gather.4
  73.6 52.9 all-gather.6
